TPU v7x, 1024 devices: a whole 4x4x32 slice. The times are simulated.
1024 devices in a mesh: dp: 32 (over z_lo, core), tp: 32 (over y, x, z_hi).
Axes of the slice: x: 4, y: 4, z: 32 (z_hi: 2, z_lo: 16; z = z_hi * 16 + z_lo), core: 2. Of those that a mesh axis runs over, the one named last changes fastest.
Arguments:
- out_grad: bfloat16 [4096, 7168], P(('dp', 'tp')), may hold values from -6 to 6
- gate_pre: bfloat16 [4096, 12288], P('dp', 'tp'), may hold values from -8 to 8
- up_pre: bfloat16 [4096, 12288], P('dp', 'tp'), may hold values from -6 to 6
- down_weight: bfloat16 [7168, 12288], P(None, 'tp'), may hold values from -0.0625 to 0.0625
- block_scales: bfloat16 [56, 96], P(None, 'tp'), may hold values from 0.25 to 4
Outputs:
- gate_grad: bfloat16 [4096, 12288], P('dp', 'tp')
- up_grad: bfloat16 [4096, 12288], P('dp', 'tp')
- down_grad: bfloat16 [7168, 12288], P('dp', 'tp')
All inputs are finite; a program needn't handle non-finite values.
Results may differ from a plain program's by a relative error of at most 0.028.
Values may be sent and summed in bfloat16 or wider, within the bound.
A program may use at most 64 MiB of HBM per device.

v0:
```python
import jax
import jax.numpy as jnp
from jax import lax
from jax.sharding import PartitionSpec as P


def tile_quant(values, tile_axis):
    largest = jnp.max(jnp.abs(values), axis=tile_axis, keepdims=True)
    tile_scale = (largest + 1e-06) / 448.0
    payload = (values / tile_scale).astype(jnp.bfloat16)
    return (payload.astype(jnp.float32) * tile_scale).astype(jnp.bfloat16)


def per_device(out_grad, gate_pre, up_pre, down_weight, block_scales):
    width = down_weight.shape[0]
    hidden_units = down_weight.shape[1]
    weight_deq = (
        down_weight.reshape(width // 128, 128, hidden_units // 128, 128)
        * block_scales[:, None, :, None]
    ).reshape(width, hidden_units)
    grad_tokens = lax.all_gather(out_grad, "tp", axis=0, tiled=True)
    local_tokens = grad_tokens.shape[0]
    grad_full = grad_tokens.astype(jnp.float32)
    grad_rowq = tile_quant(grad_full.reshape(local_tokens, width // 128, 128), 2).reshape(
        local_tokens, width
    )
    grad_colq = tile_quant(grad_full.reshape(local_tokens // 128, 128, width), 1).reshape(
        local_tokens, width
    )
    hidden_grad = jnp.dot(grad_rowq, weight_deq, preferred_element_type=jnp.float32)
    gate_val = gate_pre.astype(jnp.float32)
    up_val = up_pre.astype(jnp.float32)
    sigma = 1.0 / (1.0 + jnp.exp(-gate_val))
    gate_grad = (hidden_grad * up_val * sigma * (1.0 + gate_val * (1.0 - sigma))).astype(
        jnp.bfloat16
    )
    up_grad = (hidden_grad * gate_val * sigma).astype(jnp.bfloat16)
    hidden_val = gate_val * sigma * up_val
    hidden_colq = tile_quant(hidden_val.reshape(local_tokens // 128, 128, hidden_units), 1).reshape(
        local_tokens, hidden_units
    )
    summed = lax.psum_scatter(
        lax.dot_general(
            grad_colq, hidden_colq, (((0,), (0,)), ((), ())), preferred_element_type=jnp.float32
        ).astype(jnp.bfloat16),
        "dp",
        scatter_dimension=0,
        tiled=True,
    )
    return (gate_grad, up_grad, summed)


def solution(mesh):
    placed = (P(("dp", "tp"), None), P("dp", "tp"), P("dp", "tp"), P(None, "tp"), P(None, "tp"))
    return jax.shard_map(
        per_device,
        mesh=mesh,
        in_specs=placed,
        out_specs=(P("dp", "tp"), P("dp", "tp"), P("dp", "tp")),
        check_vma=False,
    )
```

profile of v0, /device:TPU:30, one launch (start us, length us, event | category | flops | bytes accessed | tf_op | source)
XLA Modules:
  0.0 606.7 jit_solution(662917795738832313)
XLA Ops:
  7.2 0.0 all-gather.3.cloned.1.call-start
  7.2 0.7 all-gather.3.cloned.1.call-update
  7.9 0.0 reduce-scatter.2.cloned.1.call-start
  7.9 8.2 %copy.10 = bf16[7168,384]{0,1:T(8,128)(2,1)} copy(bf16[7168,384]{1,0:T(8,128)(2,1)} %param.8) | data formatting | bytes 11010048 | tf_op args[3]
  16.1 204.8 %all-gather.3.cloned.1.call-done = bf16[32,4,7168]{2,1,0:T(4,128)(2,1)} async-done(((bf16[1,4,7168]{2,1,0:T(4,128)(2,1)}), bf16[32,4,7168]{2,1,0:T(4,128)(2,1)}) %all-gather.3.cloned.1.call-update) | async-done | bytes 1835024 | tf_op jit(solution)/shard_map/all_gather | solution.py:21
  220.9 4.3 reshape.63
  225.3 2.5 abs_reduce_fusion
  227.8 2.5 copy.11
  230.3 0.0 copy-start.1
  230.3 3.1 reduce_max.27
  233.4 1.0 div.52
  234.4 0.0 copy-start
  234.4 0.0 copy-start.2
  234.4 0.0 copy-start.3
  234.4 0.0 copy-done.1
  234.4 0.8 mul.57
  235.2 1.2 copy-done
  236.4 0.0 copy-done.2
  236.4 0.0 copy-done.3
  236.4 5.2 fusion.14
  241.7 4.0 convolution_convert_fusion
  245.7 0.0 reduce-scatter.2.cloned.1.call-update
  245.7 354.1 %reduce-scatter.2.cloned.1.call-done = bf16[224,384]{1,0:T(8,128)(2,1)} async-done(((bf16[7168,384]{1,0:T(8,128)(2,1)}), bf16[224,384]{1,0:T(8,128)(2,1)}) %reduce-scatter.2.cloned.1.call-update) | async-done | bytes 172048 | tf_op jit(solution)/shard_map/reduce_scatter | solution.py:42
  (3 shorter events, 0.0 us)
Async XLA Ops:
  7.2 213.8 %all-gather.3.cloned.1.call-start = ((), (), s32[]{:S(2)}) async-start(), calls=%async_computation.2 | async-start | bytes 1892352 | tf_op jit(solution)/shard_map/all_gather | solution.py:21
  7.9 591.9 %reduce-scatter.2.cloned.1.call-start = ((), (), s32[]{:S(2)}) async-start(), calls=%async_computation.1 | async-start | bytes 5677056 | tf_op jit(solution)/shard_map/reduce_scatter | solution.py:42
  230.3 4.1 copy-start.1
  234.4 2.0 copy-start
  234.4 2.0 copy-start.2
  234.4 2.0 copy-start.3
Sparse Core Ops, SparseCore 0:
  13.8 207.1 all-gather.2
  245.9 353.9 reduce-scatter.1
where the time goes:
time: 607 us
  waiting for transfers between devices  560 us (92%)
  local copies, waits for them, and re-layouts  18 us (3%)
  between operations  14.1 us (2%)
  matrix products  9.28 us (2%)
    reduce_scatter x1, waiting for transfers between devices, per_device(): lax.psum_scatter(lax.dot_general(grad_colq, hidden_colq, (((0,), (0,)), (...  354 us
    all_gather x1, waiting for transfers between devices, per_device(): grad_tokens = lax.all_gather(out_grad, 'tp', axis=0, tiled=True)  205 us
  transfers between devices with their start and end apart: 2, of which 2 were waited for; matrix products, arithmetic and copies ran while one was open for 1% of the time, Pallas kernels for 0%

commit v1 on v0

v1 whole, which is shorter than its diff:
```python
import jax
import jax.numpy as jnp
from jax import lax
from jax.experimental import pallas as pl
from jax.experimental.pallas import tpu as pltpu
from jax.sharding import PartitionSpec as P

F32, BF16 = jnp.float32, jnp.bfloat16
D, FFL, TOK = 7168, 384, 128
HALF = D // 2
RING, LINE, REACH = 4, 16, 8
PIECE = HALF // 2
ROWS = 224


def kernel(
    og_ref, gsrc_ref, gate_ref, up_ref, scale_ref, w_hbm,
    gg_ref, ug_ref, dg_ref,
    g1, g1relay, hid, gblk, relay_p, relay_m, g2, g2d, w, acc, dacc,
    hid_recv, hid_send, hid_left, part_send,
    xy_recv, xy_send, blk_recv, near_send, far_send, far_recv, fan_send, anti_sem, w_sem, own_sem,
):
    d = lax.axis_index("dp")
    t = lax.axis_index("tp")
    z, c = d // 2, lax.rem(d, 2)
    h = lax.rem(t, 2)
    q0 = t // 2
    y0, x0 = q0 // RING, lax.rem(q0, RING)
    zf = h * LINE + z
    step_dir = 1 - 2 * c

    def along_z(delta, core):
        pos = lax.rem(zf + delta + 2 * LINE, 2 * LINE)
        return {"dp": lax.rem(pos, LINE) * 2 + core, "tp": q0 * 2 + pos // LINE}

    def in_plane(x, y):
        return {"tp": (y * RING + x) * 2 + h}

    def wrap(v):
        return lax.rem(v + 2 * RING, RING)

    partner = {"dp": d + step_dir}

    def remote(src, dst, ssem, rsem, device):
        return pltpu.make_async_remote_copy(
            src_ref=src, dst_ref=dst, send_sem=ssem, recv_sem=rsem,
            device_id=device, device_id_type=pl.DeviceIdType.MESH,
        )

    barrier = pltpu.get_barrier_semaphore()

    def greet(device):
        pl.semaphore_signal(barrier, inc=1, device_id=device, device_id_type=pl.DeviceIdType.MESH)

    def greet_z(i, carry):
        for core in (0, 1):
            greet(along_z(i, core))
            greet(along_z(-i, core))
        return carry

    lax.fori_loop(1, REACH + 1, greet_z, 0)
    greet(partner)
    for off in (-1, 1):
        greet(in_plane(wrap(x0 + off), y0))
        greet(in_plane(x0, wrap(y0 + off)))
    w_copy = pltpu.make_async_copy(w_hbm, w, w_sem)
    w_copy.start()
    own_copy = pltpu.make_async_copy(og_ref, g1.at[q0, h], own_sem.at[0])
    own_copy.start()
    pl.semaphore_wait(barrier, 4 * REACH + 5)

    def half_rows(half):
        return pl.ds(half * (ROWS // 2), ROWS // 2)

    def unit(k, half, q):
        if k == 2:
            return g2.at[q, half_rows(half)]
        hh = h if k == 0 else 1 - h
        return g1.at[q, hh, :, pl.ds(half * PIECE, PIECE)]

    def own_unit(k, half):
        if k == 0:
            return og_ref.at[:, pl.ds(half * PIECE, PIECE)]
        return unit(k, half, q0)

    def q_of(half, p, s):
        return s * RING + p if half == 0 else p * RING + s

    def dev_of(half, p, s):
        return in_plane(p, s) if half == 0 else in_plane(s, p)

    def xy_send_unit(k, half, idx, q, device, src=None):
        remote(
            unit(k, half, q) if src is None else src, unit(k, half, q),
            xy_send.at[k, half, idx], xy_recv.at[k, half, q], device,
        ).start()

    def xy_wait(k, half, q):
        u = unit(k, half, q)
        remote(u, u, xy_send.at[k, half, 0], xy_recv.at[k, half, q], partner).wait_recv()

    def pos(half):
        return (x0, y0) if half == 0 else (y0, x0)

    def xy_start(k):
        for half in (0, 1):
            p, s = pos(half)
            src = own_unit(k, half)
            pf, pb = wrap(p + step_dir), wrap(p - step_dir)
            sf, sb = wrap(s + step_dir), wrap(s - step_dir)
            xy_send_unit(k, half, 0, q0, dev_of(half, pf, s), src)
            xy_send_unit(k, half, 1, q0, dev_of(half, pb, s), src)
            xy_send_unit(k, half, 2, q0, dev_of(half, p, sf), src)
            xy_send_unit(k, half, 3, q0, dev_of(half, p, sb), src)

    def xy_first(k):
        for stage in (0, 1, 2):
            for half in (0, 1):
                p, s = pos(half)
                pf, pb, po = wrap(p + step_dir), wrap(p - step_dir), wrap(p + 2)
                sf, sb = wrap(s + step_dir), wrap(s - step_dir)
                q = q_of(half, (pb, pf, po)[stage], s)
                xy_wait(k, half, q)
                if stage == 0:
                    xy_send_unit(k, half, 4, q, dev_of(half, pf, s))
                xy_send_unit(k, half, 5 + 2 * stage, q, dev_of(half, p, sf))
                xy_send_unit(k, half, 6 + 2 * stage, q, dev_of(half, p, sb))

    def columns_of(p):
        return (p, wrap(p - step_dir), wrap(p + step_dir), wrap(p + 2))

    def xy_second(k):
        for i in range(RING):
            for half in (0, 1):
                p, s = pos(half)
                sf, sb = wrap(s + step_dir), wrap(s - step_dir)
                q = q_of(half, columns_of(p)[i], sb)
                xy_wait(k, half, q)
                xy_send_unit(k, half, 11 + i, q, dev_of(half, p, sf))

    def xy_last(k):
        for i in range(RING):
            for half in (0, 1):
                p, s = pos(half)
                xy_wait(k, half, q_of(half, columns_of(p)[i], wrap(s + step_dir)))
        for i in range(RING):
            for half in (0, 1):
                p, s = pos(half)
                xy_wait(k, half, q_of(half, columns_of(p)[i], wrap(s + 2)))

    def xy_drain(k):
        for half in (0, 1):
            def one(i, carry, half=half):
                u = unit(k, half, q0)
                remote(u, u, xy_send.at[k, half, i], xy_recv.at[k, half, q0], partner).wait_send()
                return carry

            lax.fori_loop(0, 15, one, 0)

    peer = along_z(step_dir * REACH, c)
    leg1 = remote(og_ref, g1relay, anti_sem.at[0], anti_sem.at[1], peer)
    leg1.start()
    src_pos = lax.rem(zf - step_dir * REACH + 2 * LINE, 2 * LINE)
    leg2 = remote(g1relay, g1.at[q0, src_pos // LINE], anti_sem.at[2], anti_sem.at[3], peer)

    me_slot = (z * 2 + c) * 2 + h

    def far_copy(side):
        first = lax.rem(zf + (REACH + 1 if side == 0 else LINE) + (0 if side == 0 else 0), LINE)
        return remote(
            gsrc_ref.at[pl.ds(first * 2, 2 * REACH)], (relay_p, relay_m)[side],
            far_send.at[side], far_recv.at[side], along_z(REACH if side == 0 else -REACH, c),
        )

    for side in (0, 1):
        far_copy(side).start()
    xy_start(0)

    def near_copy(i, sign, core):
        device = along_z(sign * i, core)
        idx = ((i - 1) * 2 + (0 if sign > 0 else 1)) * 2 + core
        return remote(gsrc_ref.at[device["dp"]], gblk.at[me_slot], near_send.at[idx], blk_recv.at[me_slot], device)

    def near_start(j, carry):
        i = REACH - j
        for sign in (1, -1):
            for core in (0, 1):
                near_copy(i, sign, core).start()
        return carry

    lax.fori_loop(0, REACH, near_start, 0)
    partner_blk = remote(
        gsrc_ref.at[partner["dp"]], gblk.at[me_slot], near_send.at[4 * REACH], blk_recv.at[me_slot], partner
    )
    partner_blk.start()
    own_blk = pltpu.make_async_copy(gsrc_ref.at[d], gblk.at[me_slot], own_sem.at[1])
    own_blk.start()

    gate = gate_ref[...].astype(F32)
    up = up_ref[...].astype(F32)
    hidden = gate * (1.0 / (1.0 + jnp.exp(-gate))) * up
    hscale = (jnp.max(jnp.abs(hidden), axis=0, keepdims=True) + 1e-6) / 448.0
    payload = (hidden / hscale).astype(BF16).astype(F32)
    hid[d] = (payload * hscale).reshape(LINE, 8, FFL).astype(BF16)

    def hid_part(zz, core, sub):
        return hid.at[zz * 2 + core, pl.ds(sub * 8, 8)]

    def hid_copy(zz, core, sub, ssem, device):
        u = hid_part(zz, core, sub)
        return remote(u, u, ssem, hid_recv.at[zz * 2 + core, sub], device)

    right, left = {"dp": lax.rem(d + 2, 2 * LINE)}, {"dp": lax.rem(d + 2 * LINE - 2, 2 * LINE)}
    for sub in (0, 1):
        @pl.when(z < LINE - 1)
        def _():
            hid_copy(z, c, sub, hid_send.at[z, sub], right).start()

        @pl.when(z > 0)
        def _():
            hid_copy(z, c, sub, hid_left.at[sub], left).start()
    for sub in (0, 1):
        hid_copy(z, c, sub, part_send.at[z, sub], partner).start()

    def hid_step(s, carry):
        for sub in (0, 1):
            @pl.when(z - s >= 0)
            def _():
                hid_copy(z - s, c, sub, part_send.at[z - s, sub], partner).wait_recv()

                @pl.when(z < LINE - 1)
                def _():
                    hid_copy(z - s, c, sub, hid_send.at[z - s, sub], right).start()

                hid_copy(z - s, c, sub, part_send.at[z - s, sub], partner).start()

            @pl.when(z + s < LINE)
            def _():
                hid_copy(z + s, c, sub, part_send.at[z + s, sub], partner).wait_recv()

                @pl.when(z > 0)
                def _():
                    hid_copy(z + s, c, sub, hid_send.at[z + s, sub], left).start()

                hid_copy(z + s, c, sub, part_send.at[z + s, sub], partner).start()
        return carry

    def hid_steps(lo, hi):
        lax.fori_loop(lo, hi, hid_step, 0)

    def fan_copy(side, i, core):
        sign = 1 if side == 0 else -1
        src = lax.rem(zf - sign * REACH + 2 * LINE, 2 * LINE)
        slot = (lax.rem(src, LINE) * 2 + c) * 2 + src // LINE
        step = i + 1 if side == 0 else i - REACH
        return remote(
            (relay_p, relay_m)[side].at[i * 2 + core], gblk.at[slot],
            fan_send.at[side, i * 2 + core], blk_recv.at[slot], along_z(step, core),
        )

    def fan_out(side, act):
        last = REACH - 1 if side == 0 else 0

        def one(j, carry):
            i = REACH - 1 - j if side == 0 else j
            for core in (0, 1):
                @pl.when(jnp.logical_or(i != last, c == side))
                def _():
                    act(fan_copy(side, i, core))
            return carry

        lax.fori_loop(0, REACH, one, 0)

    low8 = lax.broadcasted_iota(jnp.int32, (LINE, 8, 128), 1) < 4

    def blocks_to_unit():
        def wait_blk(slot, carry):
            @pl.when(slot != me_slot)
            def _():
                remote(gsrc_ref.at[0], gblk.at[slot], near_send.at[0], blk_recv.at[slot], partner).wait_recv()
            return carry

        lax.fori_loop(0, 4 * LINE, wait_blk, 0)
        own_blk.wait()
        for part in (0, 1):
            v0 = gblk[pl.ds(part * 32, 32)].astype(F32).reshape(16, 2, 8, 128)
            va, vb = v0[:, 0], v0[:, 1]
            first = jnp.where(low8, va, pltpu.roll(vb, 4, 1)).reshape(128, 128)
            second = jnp.where(low8, pltpu.roll(va, 4, 1), vb).reshape(128, 128)
            g2[q0, pl.ds(0, 128), pl.ds(part * 128, 128)] = first.T.astype(BF16)
            g2[q0, pl.ds(128, 96), pl.ds(part * 128, 128)] = second.T[:96].astype(BF16)

    def row_quant(v):
        s = (jnp.max(jnp.abs(v), axis=-1, keepdims=True) + 1e-6) / 448.0
        return ((v * (1.0 / s)).astype(BF16).astype(F32) * s).astype(BF16)

    def grad_tile(l, carry):
        lanes = pl.ds(pl.multiple_of(l * 128, 128), 128)
        va = g1[:, 0, :, lanes].astype(F32)
        vb = g1[:, 1, :, lanes].astype(F32)
        first = jnp.where(low8, va, pltpu.roll(vb, 4, 1)).reshape(TOK, 128)
        second = jnp.where(low8, pltpu.roll(va, 4, 1), vb).reshape(TOK, 128)
        lhs = jnp.concatenate([row_quant(first), row_quant(second)], axis=1)
        rows = pl.ds(pl.multiple_of(l * 128, 128), 128)
        rows2 = pl.ds(pl.multiple_of(HALF + l * 128, 128), 128)
        wa = (w[rows].astype(F32) * scale_ref[pl.ds(l, 1)]).astype(BF16)
        wb = (w[rows2].astype(F32) * scale_ref[pl.ds(l + 28, 1)]).astype(BF16)
        rhs = jnp.concatenate([wa, wb], axis=0)
        acc[...] += jnp.dot(lhs, rhs, preferred_element_type=F32)
        return carry

    def grad_tiles(lo, hi):
        lax.fori_loop(lo, hi, grad_tile, 0)

    def grads_out():
        hg = acc[...]
        g = gate_ref[...].astype(F32)
        u = up_ref[...].astype(F32)
        sg = 1.0 / (1.0 + jnp.exp(-g))
        gg_ref[...] = (hg * u * sg * (1.0 + g * (1.0 - sg))).astype(BF16)
        ug_ref[...] = (hg * g * sg).astype(BF16)

    lane = lax.broadcasted_iota(jnp.int32, (16, 256), 1)

    def col_quant(i, carry):
        rows = pl.ds(pl.multiple_of(i * 16, 16), 16)
        m = jnp.abs(g2[0, rows].astype(F32))
        for q in range(1, LINE):
            m = jnp.maximum(m, jnp.abs(g2[q, rows].astype(F32)))
        for k in (1, 2, 4):
            swapped = jnp.where(lax.rem(lane // k, 2) == 0, pltpu.roll(m, 256 - k, 1), pltpu.roll(m, k, 1))
            m = jnp.maximum(m, swapped)
        s = (m + 1e-6) / 448.0
        inv = 1.0 / s
        for q in range(LINE):
            v = (g2[q, rows].astype(F32) * inv).astype(BF16).astype(F32)
            g2d[q, rows] = (v * s).astype(BF16)
        return carry

    def down_dot(q, carry):
        rhs = hid[:, q].astype(F32).reshape(256, FFL).astype(BF16)
        dacc[...] += jnp.dot(g2d[q], rhs, preferred_element_type=F32)
        return carry

    acc[...] = jnp.zeros_like(acc)
    dacc[...] = jnp.zeros_like(dacc)
    xy_first(0)
    hid_steps(1, 2)
    xy_second(0)
    hid_steps(2, 4)
    for side in (0, 1):
        far_copy(side).wait_recv()
        fan_out(side, lambda copy: copy.start())
    leg1.wait_recv()
    leg2.start()
    hid_steps(4, 7)
    xy_last(0)
    blocks_to_unit()
    xy_start(2)
    hid_steps(7, 8)
    leg2.wait_recv()
    xy_start(1)
    xy_first(2)
    hid_steps(8, 9)
    xy_first(1)
    xy_second(2)
    hid_steps(9, 11)
    xy_second(1)
    xy_last(2)
    hid_steps(11, 12)
    xy_last(1)
    own_copy.wait()
    w_copy.wait()
    grad_tiles(0, 7)
    hid_steps(12, 13)
    grad_tiles(7, 14)
    hid_steps(13, 14)
    grad_tiles(14, 21)
    hid_steps(14, 15)
    grad_tiles(21, 28)
    hid_steps(15, 16)
    lax.fori_loop(0, ROWS // 16, col_quant, 0)
    grads_out()

    def wait_other(zz, carry):
        for sub in (0, 1):
            hid_copy(zz, 1 - c, sub, part_send.at[zz, sub], partner).wait_recv()
        return carry

    lax.fori_loop(0, LINE, wait_other, 0)
    lax.fori_loop(0, LINE, down_dot, 0)
    dg_ref[...] = dacc[...].astype(BF16)

    leg1.wait_send()
    leg2.wait_send()
    for side in (0, 1):
        far_copy(side).wait_send()
        fan_out(side, lambda copy: copy.wait_send())

    def near_drain(i, carry):
        for sign in (1, -1):
            for core in (0, 1):
                near_copy(i, sign, core).wait_send()
        return carry

    lax.fori_loop(1, REACH + 1, near_drain, 0)
    partner_blk.wait_send()
    for k in (0, 1, 2):
        xy_drain(k)

    def hid_drain(zz, carry):
        for sub in (0, 1):
            hid_copy(zz, c, sub, part_send.at[zz, sub], partner).wait_send()

            @pl.when(jnp.logical_or(jnp.logical_and(zz <= z, z < LINE - 1), jnp.logical_and(zz > z, z > 0)))
            def _():
                hid_copy(zz, c, sub, hid_send.at[zz, sub], right).wait_send()
        return carry

    lax.fori_loop(0, LINE, hid_drain, 0)
    for sub in (0, 1):
        @pl.when(z > 0)
        def _():
            hid_copy(z, c, sub, hid_left.at[sub], left).wait_send()


def per_device(out_grad, gate_pre, up_pre, down_weight, block_scales):
    og = out_grad.reshape(4, 2, HALF).transpose(1, 0, 2).reshape(8, HALF)
    blocks = jnp.pad(out_grad.reshape(4, 32, ROWS), ((0, 0), (0, 0), (0, 256 - ROWS)))
    blocks = blocks.reshape(4, 32, 2, 128).transpose(1, 2, 0, 3).reshape(32, 8, 128)
    blocks = jnp.concatenate([blocks, blocks[:16]], axis=0)
    scales = jnp.repeat(block_scales.astype(F32), 128, axis=1)
    vmem = pl.BlockSpec(memory_space=pltpu.VMEM)
    dma = pltpu.SemaphoreType.DMA
    return pl.pallas_call(
        kernel,
        out_shape=(
            jax.ShapeDtypeStruct((TOK, FFL), BF16),
            jax.ShapeDtypeStruct((TOK, FFL), BF16),
            jax.ShapeDtypeStruct((ROWS, FFL), BF16),
        ),
        in_specs=[vmem] * 5 + [pl.BlockSpec(memory_space=pl.ANY)],
        out_specs=(vmem, vmem, vmem),
        scratch_shapes=[
            pltpu.VMEM((16, 2, 8, HALF), BF16),
            pltpu.VMEM((8, HALF), BF16),
            pltpu.VMEM((32, 16, 8, FFL), BF16),
            pltpu.VMEM((64, 8, 128), BF16),
            pltpu.VMEM((16, 8, 128), BF16),
            pltpu.VMEM((16, 8, 128), BF16),
            pltpu.VMEM((16, ROWS, 256), BF16),
            pltpu.VMEM((16, ROWS, 256), BF16),
            pltpu.VMEM((D, FFL), BF16),
            pltpu.VMEM((TOK, FFL), F32),
            pltpu.VMEM((ROWS, FFL), F32),
            dma((32, 2)), dma((16, 2)), dma((2,)), dma((16, 2)),
            dma((3, 2, 16)), dma((3, 2, 15)), dma((64,)), dma((33,)),
            dma((2,)), dma((2,)), dma((2, 16)), dma((4,)), dma, dma((2,)),
        ],
        compiler_params=pltpu.CompilerParams(
            collective_id=0, has_side_effects=True, vmem_limit_bytes=48 * 1024 * 1024
        ),
        name="fused_backward",
    )(og, blocks, gate_pre, up_pre, scales, down_weight)


def solution(mesh):
    placed = (P(("dp", "tp"), None), P("dp", "tp"), P("dp", "tp"), P(None, "tp"), P(None, "tp"))
    return jax.shard_map(
        per_device,
        mesh=mesh,
        in_specs=placed,
        out_specs=(P("dp", "tp"), P("dp", "tp"), P("dp", "tp")),
        check_vma=False,
    )
```

time: 607 us -> 121 us (0.20)
  the two profiles are of different devices: /device:TPU:30 before, /device:TPU:1 now
where the time goes in v1:
time: 121 us; the launch traced here: 119 us
  Pallas kernels  112 us (93%)
  local copies, waits for them, and re-layouts  6.55 us (5%)
    pallas_call x1, Pallas kernels, per_device(): pl.pallas_call(kernel, out_shape=(jax.ShapeDtypeStruct((TOK, FFL), BF16),...  112 us
    unnamed x8, local copies, waits for them, and re-layouts  3.74 us

profile of v1, /device:TPU:1, one launch (start us, length us, event | category | flops | bytes accessed | tf_op | source)
XLA Modules:
  0.0 119.3 jit_solution(4832292087027029333)
XLA Ops:
  0.6 0.8 copy.13
  1.4 0.8 reshape.26.og_ref
  2.2 0.9 reshape.27
  3.3 0.1 copy.11
  3.4 0.1 broadcast_in_dim.3
  3.5 0.0 copy-start
  3.5 0.9 copy-done
  4.4 0.0 copy-start.1
  4.4 0.9 copy-done.1
  5.3 112.0 %fused_backward.1 = (bf16[128,384]{1,0:T(8,128)(2,1)S(1)}, bf16[128,384]{1,0:T(8,128)(2,1)S(1)}, bf16[224,384]{1,0:T(8,128)(2,1)S(1)}) custom-call(bf16[8,3584]{1,0:T(8,128)(2,1)S(1)} %reshape.26.og_ref, bf16[48,8,128]{2,1,0:T(8,128)(2,1)S(1)} %pad_maximum_fusion.gsrc_ref, bf16[128,384]{1,0:T(8,128)(2,1)S(1)} %copy-done, bf16[128,384]{1,0:T(8,128)(2,1)S(1)} %copy-done.1, ...), custom_call_target="tpu_custom_call" | custom-call | tf_op jit(solution)/shard_map/fused_backward/pallas_call | solution.py:435
  117.3 0.6 copy.20
  118.0 0.6 copy.21
  118.6 0.7 copy.22
  (6 shorter events, 0.1 us)
Async XLA Ops:
  3.5 0.9 copy-start
  4.4 0.9 copy-start.1

commit v2 on v1

--- a/solution.py
+++ b/solution.py
@@ -14,11 +14,11 @@
 
 
 def kernel(
-    og_ref, gsrc_ref, gate_ref, up_ref, scale_ref, w_hbm,
+    raw_hbm, gate_hbm, up_hbm, scale_ref, w_hbm,
     gg_ref, ug_ref, dg_ref,
-    g1, g1relay, hid, gblk, relay_p, relay_m, g2, g2d, w, acc, dacc,
+    raw, gate_ref, up_ref, og_ref, gsrc_ref, g1, g1relay, hid, gblk, relay_p, relay_m, g2, g2d, w, acc, dacc,
     hid_recv, hid_send, hid_left, part_send,
-    xy_recv, xy_send, blk_recv, near_send, far_send, far_recv, fan_send, anti_sem, w_sem, own_sem,
+    xy_recv, xy_send, blk_recv, near_send, far_send, far_recv, fan_send, anti_sem, w_sem, own_sem, in_sem,
 ):
     d = lax.axis_index("dp")
     t = lax.axis_index("tp")
@@ -63,11 +63,46 @@
     for off in (-1, 1):
         greet(in_plane(wrap(x0 + off), y0))
         greet(in_plane(x0, wrap(y0 + off)))
+    fetches = [
+        pltpu.make_async_copy(src, dst, in_sem.at[i])
+        for i, (src, dst) in enumerate(((raw_hbm, raw), (gate_hbm, gate_ref), (up_hbm, up_ref)))
+    ]
+    for fetch in fetches:
+        fetch.start()
     w_copy = pltpu.make_async_copy(w_hbm, w, w_sem)
     w_copy.start()
+
+    fetches[0].wait()
+    four = raw[...].astype(F32)
+    eight = jnp.concatenate([four, four], axis=0)
+    low = lax.broadcasted_iota(jnp.int32, (8, 128), 0) < 4
+    for i in range(HALF // 128):
+        og_ref[:, i * 128:(i + 1) * 128] = jnp.where(
+            low, eight[:, i * 128:(i + 1) * 128], eight[:, HALF + i * 128:HALF + (i + 1) * 128]
+        ).astype(BF16)
+    for i in range(32):
+        base, shift = i * ROWS // 128 * 128, i * ROWS % 128
+        window = eight[:, base:min(base + 384, D)]
+        if shift:
+            window = pltpu.roll(window, window.shape[1] - shift, 1)
+        block = jnp.where(low, window[:, :128], window[:, 128:256]).astype(BF16)
+        gsrc_ref[i] = block
+        if i < LINE:
+            gsrc_ref[i + 32] = block
+
+    fetches[1].wait()
+    fetches[2].wait()
+    gate = gate_ref[...].astype(F32)
+    up = up_ref[...].astype(F32)
+    hidden = gate * (1.0 / (1.0 + jnp.exp(-gate))) * up
+    hscale = (jnp.max(jnp.abs(hidden), axis=0, keepdims=True) + 1e-6) / 448.0
+    payload = (hidden / hscale).astype(BF16).astype(F32)
+    hid[d] = (payload * hscale).reshape(LINE, 8, FFL).astype(BF16)
+    acc[...] = jnp.zeros_like(acc)
+    dacc[...] = jnp.zeros_like(dacc)
+    pl.semaphore_wait(barrier, 4 * REACH + 5)
     own_copy = pltpu.make_async_copy(og_ref, g1.at[q0, h], own_sem.at[0])
     own_copy.start()
-    pl.semaphore_wait(barrier, 4 * REACH + 5)
 
     def half_rows(half):
         return pl.ds(half * (ROWS // 2), ROWS // 2)
@@ -113,30 +148,39 @@
             xy_send_unit(k, half, 2, q0, dev_of(half, p, sf), src)
             xy_send_unit(k, half, 3, q0, dev_of(half, p, sb), src)
 
-    def xy_first(k):
-        for stage in (0, 1, 2):
-            for half in (0, 1):
-                p, s = pos(half)
-                pf, pb, po = wrap(p + step_dir), wrap(p - step_dir), wrap(p + 2)
-                sf, sb = wrap(s + step_dir), wrap(s - step_dir)
-                q = q_of(half, (pb, pf, po)[stage], s)
-                xy_wait(k, half, q)
-                if stage == 0:
-                    xy_send_unit(k, half, 4, q, dev_of(half, pf, s))
-                xy_send_unit(k, half, 5 + 2 * stage, q, dev_of(half, p, sf))
-                xy_send_unit(k, half, 6 + 2 * stage, q, dev_of(half, p, sb))
-
     def columns_of(p):
         return (p, wrap(p - step_dir), wrap(p + step_dir), wrap(p + 2))
 
-    def xy_second(k):
-        for i in range(RING):
-            for half in (0, 1):
-                p, s = pos(half)
-                sf, sb = wrap(s + step_dir), wrap(s - step_dir)
-                q = q_of(half, columns_of(p)[i], sb)
-                xy_wait(k, half, q)
-                xy_send_unit(k, half, 11 + i, q, dev_of(half, p, sf))
+    def xy_row(k, half, stage):
+        p, s = pos(half)
+        q = q_of(half, columns_of(p)[stage], s)
+        xy_wait(k, half, q)
+        if stage == 1:
+            xy_send_unit(k, half, 4, q, dev_of(half, wrap(p + step_dir), s))
+        xy_send_unit(k, half, 3 + 2 * stage, q, dev_of(half, p, wrap(s + step_dir)))
+        xy_send_unit(k, half, 4 + 2 * stage, q, dev_of(half, p, wrap(s - step_dir)))
+
+    def xy_column(k, half, i):
+        p, s = pos(half)
+        q = q_of(half, columns_of(p)[i], wrap(s - step_dir))
+        xy_wait(k, half, q)
+        xy_send_unit(k, half, 11 + i, q, dev_of(half, p, wrap(s + step_dir)))
+
+    def hop1(k):
+        for half in (0, 1):
+            xy_row(k, half, 1)
+            xy_row(k, half, 2)
+            xy_column(k, half, 0)
+
+    def hop2(k):
+        for half in (0, 1):
+            xy_row(k, half, 3)
+            xy_column(k, half, 1)
+            xy_column(k, half, 2)
+
+    def hop3(k):
+        for half in (0, 1):
+            xy_column(k, half, 3)
 
     def xy_last(k):
         for i in range(RING):
@@ -195,13 +239,6 @@
     partner_blk.start()
     own_blk = pltpu.make_async_copy(gsrc_ref.at[d], gblk.at[me_slot], own_sem.at[1])
     own_blk.start()
-
-    gate = gate_ref[...].astype(F32)
-    up = up_ref[...].astype(F32)
-    hidden = gate * (1.0 / (1.0 + jnp.exp(-gate))) * up
-    hscale = (jnp.max(jnp.abs(hidden), axis=0, keepdims=True) + 1e-6) / 448.0
-    payload = (hidden / hscale).astype(BF16).astype(F32)
-    hid[d] = (payload * hscale).reshape(LINE, 8, FFL).astype(BF16)
 
     def hid_part(zz, core, sub):
         return hid.at[zz * 2 + core, pl.ds(sub * 8, 8)]
@@ -342,45 +379,46 @@
         dacc[...] += jnp.dot(g2d[q], rhs, preferred_element_type=F32)
         return carry
 
-    acc[...] = jnp.zeros_like(acc)
-    dacc[...] = jnp.zeros_like(dacc)
-    xy_first(0)
     hid_steps(1, 2)
-    xy_second(0)
-    hid_steps(2, 4)
+    hop1(0)
+    hid_steps(2, 3)
+    hop2(0)
+    hid_steps(3, 4)
+    hop3(0)
+    leg1.wait_recv()
+    leg2.start()
     for side in (0, 1):
         far_copy(side).wait_recv()
         fan_out(side, lambda copy: copy.start())
-    leg1.wait_recv()
-    leg2.start()
     hid_steps(4, 7)
-    xy_last(0)
+    leg2.wait_recv()
+    xy_start(1)
     blocks_to_unit()
     xy_start(2)
     hid_steps(7, 8)
-    leg2.wait_recv()
-    xy_start(1)
-    xy_first(2)
+    xy_last(0)
+    hop1(1)
+    hop1(2)
     hid_steps(8, 9)
-    xy_first(1)
-    xy_second(2)
-    hid_steps(9, 11)
-    xy_second(1)
+    hop2(1)
+    hop2(2)
+    hid_steps(9, 10)
+    hop3(1)
+    hop3(2)
+    hid_steps(10, 12)
+    xy_last(1)
     xy_last(2)
-    hid_steps(11, 12)
-    xy_last(1)
     own_copy.wait()
     w_copy.wait()
-    grad_tiles(0, 7)
+    grad_tiles(0, 10)
     hid_steps(12, 13)
-    grad_tiles(7, 14)
+    grad_tiles(10, 20)
     hid_steps(13, 14)
-    grad_tiles(14, 21)
+    grad_tiles(20, 28)
+    grads_out()
     hid_steps(14, 15)
-    grad_tiles(21, 28)
+    lax.fori_loop(0, ROWS // 16, col_quant, 0)
     hid_steps(15, 16)
-    lax.fori_loop(0, ROWS // 16, col_quant, 0)
-    grads_out()
 
     def wait_other(zz, carry):
         for sub in (0, 1):
@@ -425,12 +463,9 @@
 
 
 def per_device(out_grad, gate_pre, up_pre, down_weight, block_scales):
-    og = out_grad.reshape(4, 2, HALF).transpose(1, 0, 2).reshape(8, HALF)
-    blocks = jnp.pad(out_grad.reshape(4, 32, ROWS), ((0, 0), (0, 0), (0, 256 - ROWS)))
-    blocks = blocks.reshape(4, 32, 2, 128).transpose(1, 2, 0, 3).reshape(32, 8, 128)
-    blocks = jnp.concatenate([blocks, blocks[:16]], axis=0)
     scales = jnp.repeat(block_scales.astype(F32), 128, axis=1)
     vmem = pl.BlockSpec(memory_space=pltpu.VMEM)
+    hbm = pl.BlockSpec(memory_space=pl.ANY)
     dma = pltpu.SemaphoreType.DMA
     return pl.pallas_call(
         kernel,
@@ -439,9 +474,14 @@
             jax.ShapeDtypeStruct((TOK, FFL), BF16),
             jax.ShapeDtypeStruct((ROWS, FFL), BF16),
         ),
-        in_specs=[vmem] * 5 + [pl.BlockSpec(memory_space=pl.ANY)],
+        in_specs=[hbm] * 3 + [vmem, hbm],
         out_specs=(vmem, vmem, vmem),
         scratch_shapes=[
+            pltpu.VMEM((4, D), BF16),
+            pltpu.VMEM((TOK, FFL), BF16),
+            pltpu.VMEM((TOK, FFL), BF16),
+            pltpu.VMEM((8, HALF), BF16),
+            pltpu.VMEM((48, 8, 128), BF16),
             pltpu.VMEM((16, 2, 8, HALF), BF16),
             pltpu.VMEM((8, HALF), BF16),
             pltpu.VMEM((32, 16, 8, FFL), BF16),
@@ -455,13 +495,13 @@
             pltpu.VMEM((ROWS, FFL), F32),
             dma((32, 2)), dma((16, 2)), dma((2,)), dma((16, 2)),
             dma((3, 2, 16)), dma((3, 2, 15)), dma((64,)), dma((33,)),
-            dma((2,)), dma((2,)), dma((2, 16)), dma((4,)), dma, dma((2,)),
+            dma((2,)), dma((2,)), dma((2, 16)), dma((4,)), dma, dma((2,)), dma((3,)),
         ],
         compiler_params=pltpu.CompilerParams(
             collective_id=0, has_side_effects=True, vmem_limit_bytes=48 * 1024 * 1024
         ),
         name="fused_backward",
-    )(og, blocks, gate_pre, up_pre, scales, down_weight)
+    )(out_grad, gate_pre, up_pre, scales, down_weight)
 
 
 def solution(mesh):

time: 121 us -> 122 us (level); the launches traced: 119 us -> 122 us
  local copies, waits for them, and re-layouts: 6.55 us -> 8 us
    unnamed x8 -> x12, local copies, waits for them, and re-layouts: 3.74 us -> 7.12 us
    reshape x3 -> x0, local copies, waits for them, and re-layouts: 1.81 us -> none  [the longest x1 0.95 us: per_device(): out_grad.reshape(4, 32, ROWS)]
where the time goes in v2:
time: 122 us
  Pallas kernels  113 us (93%)
  local copies, waits for them, and re-layouts  8 us (7%)
    pallas_call x1, Pallas kernels, per_device(): pl.pallas_call(kernel, out_shape=(jax.ShapeDtypeStruct((TOK, FFL), BF16),...  113 us
    unnamed x12, local copies, waits for them, and re-layouts  7.12 us

profile of v2, /device:TPU:1, one launch (start us, length us, event | category | flops | bytes accessed | tf_op | source)
XLA Modules:
  0.0 121.9 jit_solution(14084082563734577721)
XLA Ops:
  0.6 0.8 copy.9
  1.4 0.1 broadcast_in_dim.3
  1.5 0.0 copy-start
  1.6 2.6 %copy-done = bf16[7168,384]{1,0:T(8,128)(2,1)S(1)} copy-done((bf16[7168,384]{1,0:T(8,128)(2,1)S(1)}, bf16[7168,384]{1,0:T(8,128)(2,1)}, u32[]{:S(2)}) %copy-start) | copy-done | bytes 5505048
  4.1 0.0 copy-start.1
  4.1 0.9 copy-done.1
  5.0 0.0 copy-start.2
  5.0 0.9 copy-done.2
  5.9 0.0 copy-start.3
  5.9 0.8 copy-done.3
  6.7 113.2 %fused_backward.1 = (bf16[128,384]{1,0:T(8,128)(2,1)S(1)}, bf16[128,384]{1,0:T(8,128)(2,1)S(1)}, bf16[224,384]{1,0:T(8,128)(2,1)S(1)}) custom-call(bf16[4,7168]{1,0:T(4,128)(2,1)S(1)} %copy-done.3, bf16[128,384]{1,0:T(8,128)(2,1)S(1)} %copy-done.1, bf16[128,384]{1,0:T(8,128)(2,1)S(1)} %copy-done.2, f32[56,384]{1,0:T(8,128)S(1)} %bitcast.4, ...), custom_call_target="tpu_custom_call" | custom-call | tf_op jit(solution)/shard_map/fused_backward/pallas_call | solution.py:470
  119.9 0.6 copy.16
  120.6 0.6 copy.17
  121.2 0.7 copy.18
  (1 shorter events, 0.0 us)
Async XLA Ops:
  1.5 2.6 %copy-start = (bf16[7168,384]{1,0:T(8,128)(2,1)S(1)}, bf16[7168,384]{1,0:T(8,128)(2,1)}, u32[]{:S(2)}) copy-start(bf16[7168,384]{1,0:T(8,128)(2,1)} %w_hbm.1) | copy-start | bytes 16515076
  4.1 0.9 copy-start.1
  5.0 0.9 copy-start.2
  5.9 0.8 copy-start.3

commit v3 on v2

--- a/solution.py
+++ b/solution.py
@@ -16,9 +16,9 @@
 def kernel(
     raw_hbm, gate_hbm, up_hbm, scale_ref, w_hbm,
     gg_ref, ug_ref, dg_ref,
-    raw, gate_ref, up_ref, og_ref, gsrc_ref, g1, g1relay, hid, gblk, relay_p, relay_m, g2, g2d, w, acc, dacc,
+    raw, gate_ref, up_ref, og_ref, gsrc_ref, g1, g1relay, hid, gblk, gpart, relay_p, relay_m, g2, g2d, w, acc, dacc,
     hid_recv, hid_send, hid_left, part_send,
-    xy_recv, xy_send, blk_recv, near_send, far_send, far_recv, fan_send, anti_sem, w_sem, own_sem, in_sem,
+    xy_recv, xy_send, blk_recv, part_recv, near_send, far_send, far_recv, fan_send, anti_sem, w_sem, own_sem, in_sem,
 ):
     d = lax.axis_index("dp")
     t = lax.axis_index("tp")
@@ -53,9 +53,8 @@
         pl.semaphore_signal(barrier, inc=1, device_id=device, device_id_type=pl.DeviceIdType.MESH)
 
     def greet_z(i, carry):
-        for core in (0, 1):
-            greet(along_z(i, core))
-            greet(along_z(-i, core))
+        greet(along_z(i, c))
+        greet(along_z(-i, c))
         return carry
 
     lax.fori_loop(1, REACH + 1, greet_z, 0)
@@ -97,10 +96,10 @@
     hidden = gate * (1.0 / (1.0 + jnp.exp(-gate))) * up
     hscale = (jnp.max(jnp.abs(hidden), axis=0, keepdims=True) + 1e-6) / 448.0
     payload = (hidden / hscale).astype(BF16).astype(F32)
-    hid[d] = (payload * hscale).reshape(LINE, 8, FFL).astype(BF16)
+    hid[c * LINE + z] = (payload * hscale).reshape(LINE, 8, FFL).astype(BF16)
     acc[...] = jnp.zeros_like(acc)
     dacc[...] = jnp.zeros_like(dacc)
-    pl.semaphore_wait(barrier, 4 * REACH + 5)
+    pl.semaphore_wait(barrier, 2 * REACH + 5)
     own_copy = pltpu.make_async_copy(og_ref, g1.at[q0, h], own_sem.at[0])
     own_copy.start()
 
@@ -201,13 +200,32 @@
 
             lax.fori_loop(0, 15, one, 0)
 
+    def hid_part(zz, core, sub):
+        return hid.at[core * LINE + zz, pl.ds(sub * 4, 4)]
+
+    def hid_copy(zz, core, sub, ssem, device):
+        u = hid_part(zz, core, sub)
+        return remote(u, u, ssem, hid_recv.at[zz * 2 + core, sub], device)
+
+    right, left = {"dp": lax.rem(d + 2, 2 * LINE)}, {"dp": lax.rem(d + 2 * LINE - 2, 2 * LINE)}
+    for sub in range(4):
+        @pl.when(z < LINE - 1)
+        def _():
+            hid_copy(z, c, sub, hid_send.at[z, sub], right).start()
+
+        @pl.when(z > 0)
+        def _():
+            hid_copy(z, c, sub, hid_left.at[sub], left).start()
+    for sub in range(4):
+        hid_copy(z, c, sub, part_send.at[z, sub], partner).start()
+
     peer = along_z(step_dir * REACH, c)
     leg1 = remote(og_ref, g1relay, anti_sem.at[0], anti_sem.at[1], peer)
     leg1.start()
     src_pos = lax.rem(zf - step_dir * REACH + 2 * LINE, 2 * LINE)
     leg2 = remote(g1relay, g1.at[q0, src_pos // LINE], anti_sem.at[2], anti_sem.at[3], peer)
 
-    me_slot = (z * 2 + c) * 2 + h
+    me_slot = z * 2 + h
 
     def far_copy(side):
         first = lax.rem(zf + (REACH + 1 if side == 0 else LINE) + (0 if side == 0 else 0), LINE)
@@ -220,47 +238,24 @@
         far_copy(side).start()
     xy_start(0)
 
-    def near_copy(i, sign, core):
-        device = along_z(sign * i, core)
-        idx = ((i - 1) * 2 + (0 if sign > 0 else 1)) * 2 + core
-        return remote(gsrc_ref.at[device["dp"]], gblk.at[me_slot], near_send.at[idx], blk_recv.at[me_slot], device)
+    def pair_of(zz):
+        return gsrc_ref.at[pl.ds(zz * 2, 2)]
+
+    def near_copy(i, sign):
+        idx = (i - 1) * 2 + (0 if sign > 0 else 1)
+        to = lax.rem(zf + sign * i + 2 * LINE, LINE)
+        return remote(pair_of(to), gblk.at[me_slot], near_send.at[idx], blk_recv.at[me_slot], along_z(sign * i, c))
 
     def near_start(j, carry):
-        i = REACH - j
         for sign in (1, -1):
-            for core in (0, 1):
-                near_copy(i, sign, core).start()
-        return carry
-
-    lax.fori_loop(0, REACH, near_start, 0)
-    partner_blk = remote(
-        gsrc_ref.at[partner["dp"]], gblk.at[me_slot], near_send.at[4 * REACH], blk_recv.at[me_slot], partner
-    )
-    partner_blk.start()
-    own_blk = pltpu.make_async_copy(gsrc_ref.at[d], gblk.at[me_slot], own_sem.at[1])
+            near_copy(REACH - j, sign).start()
+        return carry
+
+    own_blk = pltpu.make_async_copy(pair_of(z), gblk.at[me_slot], own_sem.at[1])
     own_blk.start()
 
-    def hid_part(zz, core, sub):
-        return hid.at[zz * 2 + core, pl.ds(sub * 8, 8)]
-
-    def hid_copy(zz, core, sub, ssem, device):
-        u = hid_part(zz, core, sub)
-        return remote(u, u, ssem, hid_recv.at[zz * 2 + core, sub], device)
-
-    right, left = {"dp": lax.rem(d + 2, 2 * LINE)}, {"dp": lax.rem(d + 2 * LINE - 2, 2 * LINE)}
-    for sub in (0, 1):
-        @pl.when(z < LINE - 1)
-        def _():
-            hid_copy(z, c, sub, hid_send.at[z, sub], right).start()
-
-        @pl.when(z > 0)
-        def _():
-            hid_copy(z, c, sub, hid_left.at[sub], left).start()
-    for sub in (0, 1):
-        hid_copy(z, c, sub, part_send.at[z, sub], partner).start()
-
     def hid_step(s, carry):
-        for sub in (0, 1):
+        for sub in range(4):
             @pl.when(z - s >= 0)
             def _():
                 hid_copy(z - s, c, sub, part_send.at[z - s, sub], partner).wait_recv()
@@ -285,14 +280,14 @@
     def hid_steps(lo, hi):
         lax.fori_loop(lo, hi, hid_step, 0)
 
-    def fan_copy(side, i, core):
+    def fan_copy(side, i):
         sign = 1 if side == 0 else -1
         src = lax.rem(zf - sign * REACH + 2 * LINE, 2 * LINE)
-        slot = (lax.rem(src, LINE) * 2 + c) * 2 + src // LINE
+        slot = lax.rem(src, LINE) * 2 + src // LINE
         step = i + 1 if side == 0 else i - REACH
         return remote(
-            (relay_p, relay_m)[side].at[i * 2 + core], gblk.at[slot],
-            fan_send.at[side, i * 2 + core], blk_recv.at[slot], along_z(step, core),
+            (relay_p, relay_m)[side].at[pl.ds(i * 2, 2)], gblk.at[slot],
+            fan_send.at[side, i], blk_recv.at[slot], along_z(step, c),
         )
 
     def fan_out(side, act):
@@ -300,32 +295,42 @@
 
         def one(j, carry):
             i = REACH - 1 - j if side == 0 else j
-            for core in (0, 1):
-                @pl.when(jnp.logical_or(i != last, c == side))
-                def _():
-                    act(fan_copy(side, i, core))
+
+            @pl.when(jnp.logical_or(i != last, c == side))
+            def _():
+                act(fan_copy(side, i))
             return carry
 
         lax.fori_loop(0, REACH, one, 0)
 
     low8 = lax.broadcasted_iota(jnp.int32, (LINE, 8, 128), 1) < 4
 
-    def blocks_to_unit():
+    swap = remote(gblk.at[:, 1 - c], gpart, near_send.at[2 * REACH], part_recv, partner)
+
+    def blocks_swap():
         def wait_blk(slot, carry):
             @pl.when(slot != me_slot)
             def _():
-                remote(gsrc_ref.at[0], gblk.at[slot], near_send.at[0], blk_recv.at[slot], partner).wait_recv()
+                remote(pair_of(0), gblk.at[slot], near_send.at[0], blk_recv.at[slot], partner).wait_recv()
             return carry
 
-        lax.fori_loop(0, 4 * LINE, wait_blk, 0)
         own_blk.wait()
-        for part in (0, 1):
-            v0 = gblk[pl.ds(part * 32, 32)].astype(F32).reshape(16, 2, 8, 128)
-            va, vb = v0[:, 0], v0[:, 1]
-            first = jnp.where(low8, va, pltpu.roll(vb, 4, 1)).reshape(128, 128)
-            second = jnp.where(low8, pltpu.roll(va, 4, 1), vb).reshape(128, 128)
-            g2[q0, pl.ds(0, 128), pl.ds(part * 128, 128)] = first.T.astype(BF16)
-            g2[q0, pl.ds(128, 96), pl.ds(part * 128, 128)] = second.T[:96].astype(BF16)
+        lax.fori_loop(0, 2 * LINE, wait_blk, 0)
+        swap.start()
+
+    def side_to_unit(blocks, core):
+        v0 = blocks.astype(F32).reshape(LINE, 2, 8, 128)
+        va, vb = v0[:, 0], v0[:, 1]
+        first = jnp.where(low8, va, pltpu.roll(vb, 4, 1)).reshape(128, 128)
+        second = jnp.where(low8, pltpu.roll(va, 4, 1), vb).reshape(128, 128)
+        lanes = pl.ds(pl.multiple_of(core * 128, 128), 128)
+        g2[q0, pl.ds(0, 128), lanes] = first.T.astype(BF16)
+        g2[q0, pl.ds(128, 96), lanes] = second.T[:96].astype(BF16)
+
+    def blocks_to_unit():
+        side_to_unit(gblk[:, c], c)
+        swap.wait_recv()
+        side_to_unit(gpart[...], 1 - c)
 
     def row_quant(v):
         s = (jnp.max(jnp.abs(v), axis=-1, keepdims=True) + 1e-6) / 448.0
@@ -374,16 +379,23 @@
             g2d[q, rows] = (v * s).astype(BF16)
         return carry
 
-    def down_dot(q, carry):
-        rhs = hid[:, q].astype(F32).reshape(256, FFL).astype(BF16)
-        dacc[...] += jnp.dot(g2d[q], rhs, preferred_element_type=F32)
+    def down_dot(j, carry):
+        total = dacc[...]
+        for i in range(4):
+            q = j * 4 + i
+            rhs = hid[:, q].astype(F32).reshape(256, FFL).astype(BF16)
+            total += jnp.dot(g2d[q], rhs, preferred_element_type=F32)
+        dacc[...] = total
         return carry
 
     hid_steps(1, 2)
+    lax.fori_loop(0, 3, near_start, 0)
     hop1(0)
     hid_steps(2, 3)
+    lax.fori_loop(3, 5, near_start, 0)
     hop2(0)
     hid_steps(3, 4)
+    lax.fori_loop(5, 8, near_start, 0)
     hop3(0)
     leg1.wait_recv()
     leg2.start()
@@ -391,6 +403,7 @@
         far_copy(side).wait_recv()
         fan_out(side, lambda copy: copy.start())
     hid_steps(4, 7)
+    blocks_swap()
     leg2.wait_recv()
     xy_start(1)
     blocks_to_unit()
@@ -405,28 +418,30 @@
     hid_steps(9, 10)
     hop3(1)
     hop3(2)
-    hid_steps(10, 12)
-    xy_last(1)
-    xy_last(2)
+    hid_steps(10, 11)
     own_copy.wait()
     w_copy.wait()
-    grad_tiles(0, 10)
+    xy_last(1)
+    grad_tiles(0, 7)
+    hid_steps(11, 12)
+    grad_tiles(7, 14)
     hid_steps(12, 13)
-    grad_tiles(10, 20)
+    grad_tiles(14, 21)
     hid_steps(13, 14)
-    grad_tiles(20, 28)
-    grads_out()
+    grad_tiles(21, 28)
     hid_steps(14, 15)
+    xy_last(2)
     lax.fori_loop(0, ROWS // 16, col_quant, 0)
     hid_steps(15, 16)
+    grads_out()
 
     def wait_other(zz, carry):
-        for sub in (0, 1):
+        for sub in range(4):
             hid_copy(zz, 1 - c, sub, part_send.at[zz, sub], partner).wait_recv()
         return carry
 
     lax.fori_loop(0, LINE, wait_other, 0)
-    lax.fori_loop(0, LINE, down_dot, 0)
+    lax.fori_loop(0, LINE // 4, down_dot, 0)
     dg_ref[...] = dacc[...].astype(BF16)
 
     leg1.wait_send()
@@ -437,17 +452,16 @@
 
     def near_drain(i, carry):
         for sign in (1, -1):
-            for core in (0, 1):
-                near_copy(i, sign, core).wait_send()
+            near_copy(i, sign).wait_send()
         return carry
 
     lax.fori_loop(1, REACH + 1, near_drain, 0)
-    partner_blk.wait_send()
+    swap.wait_send()
     for k in (0, 1, 2):
         xy_drain(k)
 
     def hid_drain(zz, carry):
-        for sub in (0, 1):
+        for sub in range(4):
             hid_copy(zz, c, sub, part_send.at[zz, sub], partner).wait_send()
 
             @pl.when(jnp.logical_or(jnp.logical_and(zz <= z, z < LINE - 1), jnp.logical_and(zz > z, z > 0)))
@@ -456,7 +470,7 @@
         return carry
 
     lax.fori_loop(0, LINE, hid_drain, 0)
-    for sub in (0, 1):
+    for sub in range(4):
         @pl.when(z > 0)
         def _():
             hid_copy(z, c, sub, hid_left.at[sub], left).wait_send()
@@ -485,7 +499,8 @@
             pltpu.VMEM((16, 2, 8, HALF), BF16),
             pltpu.VMEM((8, HALF), BF16),
             pltpu.VMEM((32, 16, 8, FFL), BF16),
-            pltpu.VMEM((64, 8, 128), BF16),
+            pltpu.VMEM((32, 2, 8, 128), BF16),
+            pltpu.VMEM((32, 8, 128), BF16),
             pltpu.VMEM((16, 8, 128), BF16),
             pltpu.VMEM((16, 8, 128), BF16),
             pltpu.VMEM((16, ROWS, 256), BF16),
@@ -493,9 +508,9 @@
             pltpu.VMEM((D, FFL), BF16),
             pltpu.VMEM((TOK, FFL), F32),
             pltpu.VMEM((ROWS, FFL), F32),
-            dma((32, 2)), dma((16, 2)), dma((2,)), dma((16, 2)),
-            dma((3, 2, 16)), dma((3, 2, 15)), dma((64,)), dma((33,)),
-            dma((2,)), dma((2,)), dma((2, 16)), dma((4,)), dma, dma((2,)), dma((3,)),
+            dma((32, 4)), dma((16, 4)), dma((4,)), dma((16, 4)),
+            dma((3, 2, 16)), dma((3, 2, 15)), dma((32,)), dma, dma((17,)),
+            dma((2,)), dma((2,)), dma((2, 8)), dma((4,)), dma, dma((2,)), dma((3,)),
         ],
         compiler_params=pltpu.CompilerParams(
             collective_id=0, has_side_effects=True, vmem_limit_bytes=48 * 1024 * 1024

time: 122 us -> 116 us (0.951)
  Pallas kernels: 113 us -> 107 us
    pallas_call x1, Pallas kernels: 113 us -> 107 us  [per_device(): pl.pallas_call(kernel, out_shape=(jax.ShapeDtypeStruct((TOK, FFL), BF16),...]
where the time goes in v3:
time: 116 us; the launch traced here: 115 us
  Pallas kernels  107 us (92%)
  local copies, waits for them, and re-layouts  8 us (7%)
    pallas_call x1, Pallas kernels, per_device(): pl.pallas_call(kernel, out_shape=(jax.ShapeDtypeStruct((TOK, FFL), BF16),...  107 us
    unnamed x12, local copies, waits for them, and re-layouts  7.12 us

profile of v3, /device:TPU:1, one launch (start us, length us, event | category | flops | bytes accessed | tf_op | source)
XLA Modules:
  0.0 115.4 jit_solution(6584074834862529219)
XLA Ops:
  0.6 0.8 copy.9
  1.4 0.1 broadcast_in_dim.3
  1.5 0.0 copy-start
  1.6 2.6 %copy-done = bf16[7168,384]{1,0:T(8,128)(2,1)S(1)} copy-done((bf16[7168,384]{1,0:T(8,128)(2,1)S(1)}, bf16[7168,384]{1,0:T(8,128)(2,1)}, u32[]{:S(2)}) %copy-start) | copy-done | bytes 5505048
  4.1 0.0 copy-start.1
  4.1 0.9 copy-done.1
  5.0 0.0 copy-start.2
  5.0 0.9 copy-done.2
  5.9 0.0 copy-start.3
  5.9 0.8 copy-done.3
  6.7 106.7 %fused_backward.1 = (bf16[128,384]{1,0:T(8,128)(2,1)S(1)}, bf16[128,384]{1,0:T(8,128)(2,1)S(1)}, bf16[224,384]{1,0:T(8,128)(2,1)S(1)}) custom-call(bf16[4,7168]{1,0:T(4,128)(2,1)S(1)} %copy-done.3, bf16[128,384]{1,0:T(8,128)(2,1)S(1)} %copy-done.1, bf16[128,384]{1,0:T(8,128)(2,1)S(1)} %copy-done.2, f32[56,384]{1,0:T(8,128)S(1)} %bitcast.4, ...), custom_call_target="tpu_custom_call" | custom-call | tf_op jit(solution)/shard_map/fused_backward/pallas_call | solution.py:484
  113.4 0.6 copy.16
  114.1 0.6 copy.17
  114.7 0.7 copy.18
  (1 shorter events, 0.0 us)
Async XLA Ops:
  1.5 2.6 %copy-start = (bf16[7168,384]{1,0:T(8,128)(2,1)S(1)}, bf16[7168,384]{1,0:T(8,128)(2,1)}, u32[]{:S(2)}) copy-start(bf16[7168,384]{1,0:T(8,128)(2,1)} %w_hbm.1) | copy-start | bytes 16515076
  4.1 0.9 copy-start.1
  5.0 0.9 copy-start.2
  5.9 0.8 copy-start.3
